TPU v7x, 32 devices: a whole 2x2x4 slice. The times are simulated.
32 devices in a mesh: expert: 4 (over y, x), dp: 8 (over z, core).
Axes of the slice: x: 2, y: 2, z: 4, core: 2. Of those that a mesh axis runs over, the one named last changes fastest.
Arguments:
- tokens: bfloat16 [512, 3072], P(('expert', 'dp')), may hold values from -6 to 6
- cotangent: bfloat16 [512, 3072], P(('expert', 'dp')), may hold values from -6 to 6
- experts: int32 [512, 2], P(('expert', 'dp')), may hold values from 0 to 3, all different within a row; in each aligned block of 16 rows (0 to 15, 16 to 31, ...) at most 8 rows name the same one
- gate_weights: float32 [512, 2], P(('expert', 'dp')), may hold values from 0.1 to 1
- w_up: bfloat16 [4, 3072, 8192], P('expert', None, 'dp'), may hold values from -0.109375 to 0.109375
- master: float32 [4, 8192, 3072], P(None, 'dp', 'expert'), may hold values from -6 to 6
- moment_one: bfloat16 [4, 8192, 3072], P(None, 'dp', 'expert'), may hold values from -18 to 18
- moment_two: bfloat16 [4, 8192, 3072], P(None, 'dp', 'expert'), may hold values from 10 to 100
Outputs:
- new_master: float32 [4, 8192, 3072], P('expert', 'dp')
Inputs may be any that keep to these rules, and one draw needn't show every extreme that they name: Each token names two different experts; the tokens of one device name any expert at most 8 times, a bound that some block reaches.
All inputs are finite; a program needn't handle non-finite values.
Results may differ from a plain program's by a relative error of at most 0.0003.
Values may be sent and summed in bfloat16 or wider, within the bound.
No kernel may reach another device: no remote copies, remote signals or barrier semaphores. Data moves between devices by JAX's collectives and lax.ppermute only.
A program may use at most 192 MiB of HBM per device.

v0:
```python
import jax
import jax.numpy as jnp
from jax import lax
from jax.sharding import PartitionSpec as P

CAP = 8
beta_one = 0.9
beta_two = 0.95
corr_one = 1.0 - (0.9**50) ** 2
corr_two = 1.0 - (0.95**50) ** 2
learn_rate = 0.2
weight_decay = 0.1
epsilon = 1e-08


def adam_update(master, moment_one, moment_two, gradient):
    first = beta_one * moment_one.astype(jnp.float32) + (1.0 - beta_one) * gradient
    second = beta_two * moment_two.astype(jnp.float32) + (1.0 - beta_two) * gradient * gradient
    update = first / corr_one / (jnp.sqrt(second / corr_two) + epsilon)
    return master - learn_rate * (update + weight_decay * master)


def body(tokens, cotangent, experts, gate_weights, w_up, master, moment_one, moment_two):
    count_experts = master.shape[0]
    model_width = tokens.shape[1]
    choices_each = experts.shape[1]
    flat_ids = experts.reshape(-1)
    onehot = (flat_ids[:, None] == jnp.arange(count_experts, dtype=jnp.int32)[None, :]).astype(
        jnp.int32
    )
    position = jnp.sum((jnp.cumsum(onehot, axis=0) - 1) * onehot, axis=1)
    target = flat_ids * CAP + position
    placing = (jnp.arange(count_experts * CAP, dtype=jnp.int32)[:, None] == target[None, :]).astype(
        jnp.bfloat16
    )
    token_copies = jnp.repeat(tokens, choices_each, axis=0)
    scaled = (
        jnp.repeat(cotangent.astype(jnp.float32), choices_each, axis=0)
        * gate_weights.reshape(-1)[:, None]
    ).astype(jnp.bfloat16)
    send_tokens = jnp.dot(placing, token_copies, preferred_element_type=jnp.float32).astype(
        jnp.bfloat16
    )
    send_scaled = jnp.dot(placing, scaled, preferred_element_type=jnp.float32).astype(jnp.bfloat16)
    send_tokens = send_tokens.reshape(count_experts, CAP, model_width)
    send_scaled = send_scaled.reshape(count_experts, CAP, model_width)
    got_tokens, got_scaled = (
        lax.all_to_all(send_tokens, "expert", split_axis=0, concat_axis=0, tiled=True),
        lax.all_to_all(send_scaled, "expert", split_axis=0, concat_axis=0, tiled=True),
    )
    got_tokens = got_tokens.reshape(-1, model_width)
    got_scaled = got_scaled.reshape(-1, model_width)
    local_up = w_up[0]
    piece_tokens = lax.all_gather(got_tokens, "dp", axis=0, tiled=True)
    piece_scaled = lax.all_gather(got_scaled, "dp", axis=0, tiled=True)
    hidden = jax.nn.silu(
        jnp.dot(piece_tokens, local_up, preferred_element_type=jnp.float32)
    ).astype(jnp.bfloat16)
    gradient = lax.dot_general(
        hidden, piece_scaled, (((0,), (0,)), ((), ())), preferred_element_type=jnp.float32
    )
    gradient = gradient[None]
    whole_master = lax.all_to_all(master, "expert", split_axis=0, concat_axis=2, tiled=True)
    first_moment, second_moment = (
        lax.all_to_all(moment_one, "expert", split_axis=0, concat_axis=2, tiled=True),
        lax.all_to_all(moment_two, "expert", split_axis=0, concat_axis=2, tiled=True),
    )
    return adam_update(whole_master, first_moment, second_moment, gradient)


def solution(mesh):
    placed = (
        P(("expert", "dp"), None),
        P(("expert", "dp"), None),
        P(("expert", "dp"), None),
        P(("expert", "dp"), None),
        P("expert", None, "dp"),
        P(None, "dp", "expert"),
        P(None, "dp", "expert"),
        P(None, "dp", "expert"),
    )
    return jax.shard_map(
        body, mesh=mesh, in_specs=placed, out_specs=P("expert", "dp", None), check_vma=False
    )
```

profile of v0, /device:TPU:0, one launch (start us, length us, event | category | flops | bytes accessed | tf_op | source)
XLA Modules:
  0.0 383.2 jit_solution(6058659593912855117)
XLA Ops:
  6.5 0.9 copy.16
  7.9 1.0 broadcast_in_dim.4
  8.9 0.9 fusion.8
  9.8 5.2 %all-to-all-start.2 = ((bf16[4,8,3072]{2,1,0:T(8,128)(2,1)}), bf16[4,8,3072]{2,1,0:T(8,128)(2,1)S(1)}, u32[]{:S(2)}, u32[]{:S(2)}) async-start(bf16[4,8,3072]{2,1,0:T(8,128)(2,1)} %fusion.8), calls=%async_computation.2 | async-start | bytes 393216 | tf_op jit(solution)/shard_map/all_to_all | solution.py:48
  15.0 0.8 copy.17
  15.8 1.0 broadcast_in_dim.5
  17.4 2.8 all-to-all-done.2
  20.2 8.6 %all_to_all.46 = bf16[4,8,3072]{2,1,0:T(8,128)(2,1)} all-to-all(bf16[4,8,3072]{2,1,0:T(8,128)(2,1)S(1)} %fusion.9), channel_id=1, replica_groups=mesh['expert'=4,'dp'=8] {'expert'}, dimensions={0} | all-to-all | bytes 393216 | tf_op jit(solution)/shard_map/all_to_all | solution.py:49
  28.8 75.0 %all_to_all.47 = bf16[4,1024,768]{2,1,0:T(8,128)(2,1)} all-to-all(bf16[4,1024,768]{2,1,0:T(8,128)(2,1)} %param.14), channel_id=1, replica_groups=mesh['expert'=4,'dp'=8] {'expert'}, dimensions={0} | all-to-all | bytes 12582912 | tf_op jit(solution)/shard_map/all_to_all | solution.py:65
  103.8 70.4 %all_to_all.48 = bf16[4,1024,768]{2,1,0:T(8,128)(2,1)} all-to-all(bf16[4,1024,768]{2,1,0:T(8,128)(2,1)S(1)} %bitcast.47), channel_id=1, replica_groups=mesh['expert'=4,'dp'=8] {'expert'}, dimensions={0} | all-to-all | bytes 12582912 | tf_op jit(solution)/shard_map/all_to_all | solution.py:66
  174.2 6.3 %all-to-all-start = ((f32[4,1024,768]{2,1,0:T(8,128)}), f32[4,1024,768]{2,1,0:T(8,128)}, u32[]{:S(2)}, u32[]{:S(2)}) async-start(f32[4,1024,768]{2,1,0:T(8,128)} %param.13), calls=%async_computation | async-start | bytes 25165824 | tf_op jit(solution)/shard_map/all_to_all | solution.py:63
  181.3 0.7 all-gather.5.cloned.1.call-update
  182.0 27.9 %all-gather.3.cloned.1.call-done = bf16[256,3072]{1,0:T(8,128)(2,1)} async-done(((bf16[32,3072]{1,0:T(8,128)(2,1)}), bf16[256,3072]{1,0:T(8,128)(2,1)}) %all-gather.3.cloned.1.call-update) | async-done | bytes 1572880 | tf_op jit(solution)/shard_map/all_gather | solution.py:54
  209.9 26.1 %all-gather.5.cloned.1.call-done = bf16[256,3072]{1,0:T(8,128)(2,1)} async-done(((bf16[32,3072]{1,0:T(8,128)(2,1)}), bf16[256,3072]{1,0:T(8,128)(2,1)}) %all-gather.5.cloned.1.call-update) | async-done | bytes 1572880 | tf_op jit(solution)/shard_map/all_gather | solution.py:55
  236.0 11.7 %fusion.13 = f32[1024,3072]{1,0:T(8,128)} fusion(bf16[256,3072]{1,0:T(8,128)(2,1)} %all-gather.5.cloned.1.call-done, bf16[256,3072]{1,0:T(8,128)(2,1)} %all-gather.3.cloned.1.call-done, bf16[1,3072,1024]{2,1,0:T(8,128)(2,1)} %param.12), kind=kOutput, calls=%fused_computation.17 | convolution fusion | flops 3222536192 | bytes 22020096 | tf_op jit(solution)/shard_map/dot_general | solution.py:59
  247.7 4.0 %multiply_bitcast_fusion = f32[1,1024,4,768]{3,1,2,0:T(8,128)S(1)} fusion(bf16[4,1024,768]{2,1,0:T(8,128)(2,1)} %all_to_all.48), kind=kLoop, calls=%fused_computation.8 | loop fusion | flops 6291456 | bytes 18874368 | tf_op jit(solution)/shard_map/mul | solution.py:18
  251.7 23.5 %copy.18 = f32[1,1024,4,768]{3,2,1,0:T(4,128)} copy(f32[1,1024,4,768]{3,1,2,0:T(8,128)S(1)} %multiply_bitcast_fusion) | data formatting | bytes 25165824 | tf_op jit(solution)/shard_map/mul | solution.py:18
  275.2 12.3 %copy.21 = f32[128,8,4,768]{3,1,2,0:T(8,128)} copy(f32[128,8,4,768]{3,2,1,0:T(4,128)} %bitcast.38) | data formatting | bytes 25165824
  287.5 1.2 multiply_bitcast_fusion.1
  288.7 23.5 %copy.15 = f32[1,1024,4,768]{3,2,1,0:T(4,128)} copy(f32[1,1024,4,768]{3,1,2,0:T(8,128)S(1)} %multiply_bitcast_fusion.1) | data formatting | bytes 25165824 | tf_op jit(solution)/shard_map/mul | solution.py:17
  312.2 12.0 %copy.20 = f32[128,8,4,768]{3,1,2,0:T(8,128)} copy(f32[128,8,4,768]{3,2,1,0:T(4,128)} %bitcast.39) | data formatting | bytes 25165824
  324.3 16.5 %copy.14 = f32[1,1024,4,768]{3,2,1,0:T(4,128)} copy(f32[1,1024,4,768]{3,1,2,0:T(8,128)} %bitcast.1) | data formatting | bytes 25165824 | tf_op jit(solution)/shard_map/all_to_all | solution.py:63
  340.8 12.1 %copy.19 = f32[128,8,4,768]{3,1,2,0:T(8,128)} copy(f32[128,8,4,768]{3,2,1,0:T(4,128)} %bitcast.40) | data formatting | bytes 25165824
  352.8 23.6 %subtract_bitcast_fusion = f32[1,1024,3072]{2,1,0:T(8,128)} fusion(f32[1024,3072]{1,0:T(8,128)} %bitcast.43, f32[1024,3072]{1,0:T(8,128)} %bitcast.41, f32[1024,3072]{1,0:T(8,128)} %fusion.13, f32[1024,3072]{1,0:T(8,128)} %bitcast.42), kind=kLoop, calls=%fused_computation.7 | loop fusion | flops 40894464 | bytes 62914560 | tf_op jit(solution)/shard_map/sub | solution.py:20
  (25 shorter events, 1.9 us)
Async XLA Ops:
  6.5 97.2 %slice-start.2 = ((s8[6291456]{0:T(1024)(128)(4,1)}), s8[2097152]{0:T(1024)(128)(4,1)S(1)}, s32[]{:S(2)}) async-start(s8[6291456]{0:T(1024)(128)(4,1)} %bitcast.46), calls=%async_computation.9 | async-start | bytes 4194304
  9.8 10.4 %all-to-all-start.2 = ((bf16[4,8,3072]{2,1,0:T(8,128)(2,1)}), bf16[4,8,3072]{2,1,0:T(8,128)(2,1)S(1)}, u32[]{:S(2)}, u32[]{:S(2)}) async-start(bf16[4,8,3072]{2,1,0:T(8,128)(2,1)} %fusion.8), calls=%async_computation.2 | async-start | bytes 393216 | tf_op jit(solution)/shard_map/all_to_all | solution.py:48
  20.2 154.0 %copy-start = (bf16[4,8,3072]{2,1,0:T(8,128)(2,1)}, bf16[4,8,3072]{2,1,0:T(8,128)(2,1)S(1)}, u32[]{:S(2)}) copy-start(bf16[4,8,3072]{2,1,0:T(8,128)(2,1)S(1)} %all-to-all-done.2) | copy-start | bytes 589828
  28.8 75.0 %slice-start.3 = ((s8[6291456]{0:T(1024)(128)(4,1)}), s8[4194304]{0:T(1024)(128)(4,1)S(1)}, s32[]{:S(2)}) async-start(s8[6291456]{0:T(1024)(128)(4,1)} %bitcast.46), calls=%async_computation.10 | async-start | bytes 8388608
  174.2 150.1 %all-to-all-start = ((f32[4,1024,768]{2,1,0:T(8,128)}), f32[4,1024,768]{2,1,0:T(8,128)}, u32[]{:S(2)}, u32[]{:S(2)}) async-start(f32[4,1024,768]{2,1,0:T(8,128)} %param.13), calls=%async_computation | async-start | bytes 25165824 | tf_op jit(solution)/shard_map/all_to_all | solution.py:63
  180.5 29.4 %all-gather.3.cloned.1.call-start = ((), (), s32[]{:S(2)}) async-start(), calls=%async_computation.5 | async-start | bytes 1769472 | tf_op jit(solution)/shard_map/all_gather | solution.py:54
  181.3 54.7 %all-gather.5.cloned.1.call-start = ((), (), s32[]{:S(2)}) async-start(), calls=%async_computation.6 | async-start | bytes 1769472 | tf_op jit(solution)/shard_map/all_gather | solution.py:55
  251.7 35.8 %slice-start = ((s8[6291456]{0:T(1024)(128)(4,1)}), s8[4194304]{0:T(1024)(128)(4,1)S(1)}, s32[]{:S(2)}) async-start(s8[6291456]{0:T(1024)(128)(4,1)} %bitcast.44), calls=%async_computation.7 | async-start | bytes 8388608
  275.2 12.3 %slice-start.1 = ((s8[6291456]{0:T(1024)(128)(4,1)}), s8[2097152]{0:T(1024)(128)(4,1)S(1)}, s32[]{:S(2)}) async-start(s8[6291456]{0:T(1024)(128)(4,1)} %bitcast.44), calls=%async_computation.8 | async-start | bytes 4194304
Sparse Core Ops, SparseCore 0:
  183.0 26.9 all-gather.2
  211.6 24.3 all-gather.4
where the time goes:
time: 384 us; the launch traced here: 383 us
  blocking collectives  154 us (40%)
  local copies, waits for them, and re-layouts  104 us (27%)
  waiting for transfers between devices  58.2 us (15%)
  other arithmetic  29.1 us (8%)
  between operations  13.5 us (4%)
  matrix products  12.8 us (3%)
  starting transfers between devices  11.6 us (3%)
    all_to_all x1, blocking collectives, body(): lax.all_to_all(moment_one, 'expert', split_axis=0, concat_axis=2, tiled=T...  75 us
    all_to_all x1, blocking collectives, body(): lax.all_to_all(moment_two, 'expert', split_axis=0, concat_axis=2, tiled=T...  70.4 us
    unnamed x15, local copies, waits for them, and re-layouts  38.1 us
    all_gather x1, waiting for transfers between devices, body(): piece_tokens = lax.all_gather(got_tokens, 'dp', axis=0, tiled=True)  27.9 us
    all_gather x1, waiting for transfers between devices, body(): piece_scaled = lax.all_gather(got_scaled, 'dp', axis=0, tiled=True)  26.1 us
    sub x1, other arithmetic, adam_update(): return master - learn_rate * (update + weight_decay * master)  23.6 us
    mul x1, local copies, waits for them, and re-layouts, adam_update(): beta_one * moment_one.astype(jnp.float32) + (1.0 - beta_one) * gradient  23.5 us
    mul x1, local copies, waits for them, and re-layouts, adam_update(): beta_two * moment_two.astype(jnp.float32)  23.5 us
  transfers between devices with their start and end apart: 4, of which 3 were waited for; matrix products, arithmetic and copies ran while one was open for 24% of the time, Pallas kernels for 0%

commit v1 on v0

--- a/solution.py
+++ b/solution.py
@@ -51,8 +51,11 @@
     got_tokens = got_tokens.reshape(-1, model_width)
     got_scaled = got_scaled.reshape(-1, model_width)
     local_up = w_up[0]
-    piece_tokens = lax.all_gather(got_tokens, "dp", axis=0, tiled=True)
-    piece_scaled = lax.all_gather(got_scaled, "dp", axis=0, tiled=True)
+    piece_tokens, piece_scaled = jnp.split(
+        lax.all_gather(jnp.concatenate([got_tokens, got_scaled], axis=1), "dp", axis=0, tiled=True),
+        [got_tokens.shape[1]],
+        axis=1,
+    )
     hidden = jax.nn.silu(
         jnp.dot(piece_tokens, local_up, preferred_element_type=jnp.float32)
     ).astype(jnp.bfloat16)

time: 384 us -> 372 us (0.969)
  waiting for transfers between devices: 58.2 us -> 46.4 us
    all_gather x2 -> x1, waiting for transfers between devices: 54 us -> 0.01 us  [body(): lax.all_gather(jnp.concatenate([got_tokens, got_scaled], axis=1), 'dp', a...]
    all_to_all x1, waiting for transfers between devices: 0.01 us -> 43.5 us  [body(): lax.all_to_all(master, 'expert', split_axis=0, concat_axis=2, tiled=True)]
    unnamed x15 -> x13, local copies, waits for them, and re-layouts: 38.1 us -> 38.3 us
  transfers between devices with their start and end apart: 4 -> 3, of which waited for: 3 -> 2; matrix products, arithmetic and copies ran while one was open for 24% -> 25% of each run, Pallas kernels for 0% -> 0%
where the time goes in v1:
time: 372 us; the launch traced here: 371 us
  blocking collectives  153 us (41%)
  local copies, waits for them, and re-layouts  104 us (28%)
  waiting for transfers between devices  46.4 us (12%)
  other arithmetic  29.9 us (8%)
  between operations  13.5 us (4%)
  matrix products  12.8 us (3%)
  starting transfers between devices  11.5 us (3%)
    all_to_all x1, blocking collectives, body(): lax.all_to_all(moment_one, 'expert', split_axis=0, concat_axis=2, tiled=T...  75 us
    all_to_all x1, blocking collectives, body(): lax.all_to_all(moment_two, 'expert', split_axis=0, concat_axis=2, tiled=T...  70.4 us
    all_to_all x1, waiting for transfers between devices, body(): lax.all_to_all(master, 'expert', split_axis=0, concat_axis=2, tiled=True)  43.5 us
    unnamed x13, local copies, waits for them, and re-layouts  38.3 us
    sub x1, other arithmetic, adam_update(): return master - learn_rate * (update + weight_decay * master)  23.6 us
    mul x1, local copies, waits for them, and re-layouts, adam_update(): beta_one * moment_one.astype(jnp.float32) + (1.0 - beta_one) * gradient  23.5 us
    mul x1, local copies, waits for them, and re-layouts, adam_update(): beta_two * moment_two.astype(jnp.float32)  23.3 us
    all_to_all x1, local copies, waits for them, and re-layouts, body(): lax.all_to_all(master, 'expert', split_axis=0, concat_axis=2, tiled=True)  16.5 us
  transfers between devices with their start and end apart: 3, of which 2 were waited for; matrix products, arithmetic and copies ran while one was open for 25% of the time, Pallas kernels for 0%

profile of v1, /device:TPU:0, one launch (start us, length us, event | category | flops | bytes accessed | tf_op | source)
XLA Modules:
  0.0 371.4 jit_solution(393965478943945009)
XLA Ops:
  6.5 0.9 copy.16
  7.9 1.0 broadcast_in_dim.4
  8.9 0.9 fusion.8
  9.8 5.2 %all-to-all-start.2 = ((bf16[4,8,3072]{2,1,0:T(8,128)(2,1)}), bf16[4,8,3072]{2,1,0:T(8,128)(2,1)S(1)}, u32[]{:S(2)}, u32[]{:S(2)}) async-start(bf16[4,8,3072]{2,1,0:T(8,128)(2,1)} %fusion.8), calls=%async_computation.2 | async-start | bytes 393216 | tf_op jit(solution)/shard_map/all_to_all | solution.py:48
  15.0 0.8 copy.17
  15.8 1.0 broadcast_in_dim.5
  16.9 0.3 reshape.69
  17.4 2.8 all-to-all-done.2
  20.2 7.9 %all_to_all.46 = bf16[4,8,3072]{2,1,0:T(8,128)(2,1)S(1)} all-to-all(bf16[4,8,3072]{2,1,0:T(8,128)(2,1)S(1)} %fusion.9), channel_id=1, replica_groups=mesh['expert'=4,'dp'=8] {'expert'}, dimensions={0} | all-to-all | bytes 393216 | tf_op jit(solution)/shard_map/all_to_all | solution.py:49
  28.1 75.0 %all_to_all.47 = bf16[4,1024,768]{2,1,0:T(8,128)(2,1)} all-to-all(bf16[4,1024,768]{2,1,0:T(8,128)(2,1)} %param.14), channel_id=1, replica_groups=mesh['expert'=4,'dp'=8] {'expert'}, dimensions={0} | all-to-all | bytes 12582912 | tf_op jit(solution)/shard_map/all_to_all | solution.py:68
  103.1 70.4 %all_to_all.48 = bf16[4,1024,768]{2,1,0:T(8,128)(2,1)} all-to-all(bf16[4,1024,768]{2,1,0:T(8,128)(2,1)S(1)} %bitcast.45), channel_id=1, replica_groups=mesh['expert'=4,'dp'=8] {'expert'}, dimensions={0} | all-to-all | bytes 12582912 | tf_op jit(solution)/shard_map/all_to_all | solution.py:69
  173.5 6.3 %all-to-all-start = ((f32[4,1024,768]{2,1,0:T(8,128)}), f32[4,1024,768]{2,1,0:T(8,128)}, u32[]{:S(2)}, u32[]{:S(2)}) async-start(f32[4,1024,768]{2,1,0:T(8,128)} %param.13), calls=%async_computation | async-start | bytes 25165824 | tf_op jit(solution)/shard_map/all_to_all | solution.py:66
  179.9 0.8 pad_maximum_fusion
  180.7 4.0 %multiply_bitcast_fusion = f32[1,1024,4,768]{3,1,2,0:T(8,128)S(1)} fusion(bf16[4,1024,768]{2,1,0:T(8,128)(2,1)} %all_to_all.48), kind=kLoop, calls=%fused_computation.8 | loop fusion | flops 6291456 | bytes 18874368 | tf_op jit(solution)/shard_map/mul | solution.py:18
  184.7 23.3 %copy.18 = f32[1,1024,4,768]{3,2,1,0:T(4,128)} copy(f32[1,1024,4,768]{3,1,2,0:T(8,128)S(1)} %multiply_bitcast_fusion) | data formatting | bytes 25165824 | tf_op jit(solution)/shard_map/mul | solution.py:18
  208.0 12.3 %copy.21 = f32[128,8,4,768]{3,1,2,0:T(8,128)} copy(f32[128,8,4,768]{3,2,1,0:T(4,128)} %bitcast.36) | data formatting | bytes 25165824
  220.3 1.2 multiply_bitcast_fusion.1
  221.5 23.5 %copy.15 = f32[1,1024,4,768]{3,2,1,0:T(4,128)} copy(f32[1,1024,4,768]{3,1,2,0:T(8,128)S(1)} %multiply_bitcast_fusion.1) | data formatting | bytes 25165824 | tf_op jit(solution)/shard_map/mul | solution.py:17
  245.0 12.2 %copy.20 = f32[128,8,4,768]{3,1,2,0:T(8,128)} copy(f32[128,8,4,768]{3,2,1,0:T(4,128)} %bitcast.37) | data formatting | bytes 25165824
  257.1 11.7 %fusion.10 = f32[1024,3072]{1,0:T(8,128)} fusion(bf16[256,6144]{1,0:T(8,128)(2,1)} %all-gather.2.cloned.1.call-done, bf16[1,3072,1024]{2,1,0:T(8,128)(2,1)} %param.12), kind=kOutput, calls=%fused_computation.16 | convolution fusion | flops 3222536192 | bytes 22020096 | tf_op jit(solution)/shard_map/dot_general | solution.py:62
  268.9 43.5 %all-to-all-done = f32[4,1024,768]{2,1,0:T(8,128)} async-done(((f32[4,1024,768]{2,1,0:T(8,128)}), f32[4,1024,768]{2,1,0:T(8,128)}, u32[]{:S(2)}, u32[]{:S(2)}) %all-to-all-start) | async-done | bytes 12582944 | tf_op jit(solution)/shard_map/all_to_all | solution.py:66
  312.4 16.5 %copy.14 = f32[1,1024,4,768]{3,2,1,0:T(4,128)} copy(f32[1,1024,4,768]{3,1,2,0:T(8,128)} %bitcast.1) | data formatting | bytes 25165824 | tf_op jit(solution)/shard_map/all_to_all | solution.py:66
  328.9 12.1 %copy.19 = f32[128,8,4,768]{3,1,2,0:T(8,128)} copy(f32[128,8,4,768]{3,2,1,0:T(4,128)} %bitcast.38) | data formatting | bytes 25165824
  341.0 23.6 %subtract_bitcast_fusion = f32[1,1024,3072]{2,1,0:T(8,128)} fusion(f32[1024,3072]{1,0:T(8,128)} %bitcast.41, f32[1024,3072]{1,0:T(8,128)} %bitcast.39, f32[1024,3072]{1,0:T(8,128)} %fusion.10, f32[1024,3072]{1,0:T(8,128)} %bitcast.40), kind=kLoop, calls=%fused_computation.7 | loop fusion | flops 40894464 | bytes 62914560 | tf_op jit(solution)/shard_map/sub | solution.py:20
  (21 shorter events, 0.9 us)
Async XLA Ops:
  6.5 96.6 %slice-start.2 = ((s8[6291456]{0:T(1024)(128)(4,1)}), s8[2097152]{0:T(1024)(128)(4,1)S(1)}, s32[]{:S(2)}) async-start(s8[6291456]{0:T(1024)(128)(4,1)} %bitcast.44), calls=%async_computation.8 | async-start | bytes 4194304
  9.8 10.4 %all-to-all-start.2 = ((bf16[4,8,3072]{2,1,0:T(8,128)(2,1)}), bf16[4,8,3072]{2,1,0:T(8,128)(2,1)S(1)}, u32[]{:S(2)}, u32[]{:S(2)}) async-start(bf16[4,8,3072]{2,1,0:T(8,128)(2,1)} %fusion.8), calls=%async_computation.2 | async-start | bytes 393216 | tf_op jit(solution)/shard_map/all_to_all | solution.py:48
  28.1 75.0 %slice-start.3 = ((s8[6291456]{0:T(1024)(128)(4,1)}), s8[4194304]{0:T(1024)(128)(4,1)S(1)}, s32[]{:S(2)}) async-start(s8[6291456]{0:T(1024)(128)(4,1)} %bitcast.44), calls=%async_computation.9 | async-start | bytes 8388608
  173.5 138.9 %all-to-all-start = ((f32[4,1024,768]{2,1,0:T(8,128)}), f32[4,1024,768]{2,1,0:T(8,128)}, u32[]{:S(2)}, u32[]{:S(2)}) async-start(f32[4,1024,768]{2,1,0:T(8,128)} %param.13), calls=%async_computation | async-start | bytes 25165824 | tf_op jit(solution)/shard_map/all_to_all | solution.py:66
  179.8 77.3 %all-gather.2.cloned.1.call-start = ((), (), s32[]{:S(2)}) async-start(), calls=%async_computation.5 | async-start | bytes 3538944 | tf_op jit(solution)/shard_map/all_gather | solution.py:55
  184.7 35.6 %slice-start = ((s8[6291456]{0:T(1024)(128)(4,1)}), s8[4194304]{0:T(1024)(128)(4,1)S(1)}, s32[]{:S(2)}) async-start(s8[6291456]{0:T(1024)(128)(4,1)} %bitcast.42), calls=%async_computation.6 | async-start | bytes 8388608
  208.0 12.3 %slice-start.1 = ((s8[6291456]{0:T(1024)(128)(4,1)}), s8[2097152]{0:T(1024)(128)(4,1)S(1)}, s32[]{:S(2)}) async-start(s8[6291456]{0:T(1024)(128)(4,1)} %bitcast.42), calls=%async_computation.7 | async-start | bytes 4194304
Sparse Core Ops, SparseCore 0:
  182.3 39.8 all-gather.1
